TPU v7x, 512 devices: a whole 4x8x8 slice. The times are simulated.
512 devices in a mesh: tile: 128 (over x, z, y_lo), spec: 4 (over y_hi, core).
Axes of the slice: x: 4, y: 8 (y_hi: 2, y_lo: 4; y = y_hi * 4 + y_lo), z: 8, core: 2. Of those that a mesh axis runs over, the one named last changes fastest.
Arguments:
- adjoint: float32 [128, 8, 512, 128], P('spec', None, 'tile'), may hold values from -6 to 6
- section_first: bfloat16 [128, 8, 128, 128], P('tile'), may hold values from -1 to 2
- section_second: bfloat16 [128, 8, 128, 128], P('tile'), may hold values from -1 to 2
- jacobian: bfloat16 [128, 8, 128, 128], P('tile'), may hold values from -0.5 to 0.5
- pattern: int32 [128, 8, 2, 2], P('tile'), may hold values 0 or 1
- counts: int32 [128, 8], P('tile'), may hold values from 1 to 512, as said below
- courant: float32 [8, 512, 128], P(None, 'tile'), may hold values from -0.45 to 0.45
- seam_codes: int32 [128, 2], P('tile'), may hold values from 0 to 1, as said below
Outputs:
- adjoint_out: float32 [128, 8, 512, 128], P('spec', None, 'tile')
Inputs may be any that keep to these rules, and one draw needn't show every extreme that they name: The active cells of tile t and level l are the first counts[t, l] of its 4 x 128 cells in row-major order. `seam_codes`: column 0 of tile t is the code of the seam between tile t and tile t + 1, column 1 that of the seam between tile t - 1 and tile t (cyclically); a 1 means that the seam reverses the order of cells along it. `pattern`: 1 where a block is present.
All inputs are finite; a program needn't handle non-finite values.
Results may differ from a plain program's by a relative error of at most 0.004.
Values may be sent and summed in bfloat16 or wider, within the bound.
No kernel may reach another device: no remote copies, remote signals or barrier semaphores. Data moves between devices by JAX's collectives and lax.ppermute only.
A program may use at most 64 MiB of HBM per device.

v0:
```python
import jax
import jax.numpy as jnp
from jax import lax
from jax.sharding import PartitionSpec as P

NSUB = 4
section_weights = (0.4, 0.3, 0.2, 0.1)
coupling = 0.5


def passed_along(value, axis, steps):
    count = lax.axis_size(axis)
    pairs = [(source, (source + steps) % count) for source in range(count)]
    return lax.ppermute(value, axis, pairs)


def padded(block, sides, width):
    for axis, dim in sides:
        count = lax.axis_size(axis)
        forward = [(i, i + 1) for i in range(count - 1)]
        forward.append((count - 1, 0))
        backward = [(target, source) for source, target in forward]
        low = lax.ppermute(
            lax.slice_in_dim(block, block.shape[dim] - width, None, axis=dim), axis, forward
        )
        high = lax.ppermute(lax.slice_in_dim(block, 0, width, axis=dim), axis, backward)
        block = jnp.concatenate([low, block, high], axis=dim)
    return block


def transposed(matrix, field_cells):
    return jnp.einsum("lsp,slc->plc", matrix, field_cells, preferred_element_type=jnp.float32)


def section_chain(rounded, first_factor, second_factor, jac_used, offset, out_width):
    start_wide = rounded.astype(jnp.float32)
    first_y = transposed(first_factor, rounded).astype(jnp.bfloat16)
    section_u = transposed(second_factor, first_y).astype(jnp.bfloat16)
    running_sum = None
    for section in range(4):
        if section < 3:
            coupled = transposed(jac_used, section_u)
            picked = lax.dynamic_slice_in_dim(coupled, offset, out_width, 0)
        else:
            picked = transposed(lax.dynamic_slice_in_dim(jac_used, offset, out_width, 2), section_u)
        if section == 0:
            running_sum = section_weights[0] * picked
        else:
            running_sum = running_sum + section_weights[section] * picked
        if section < 3:
            mixed_term = (start_wide + coupling * coupled).astype(jnp.bfloat16)
            first_y = transposed(first_factor, mixed_term).astype(jnp.bfloat16)
            section_u = transposed(second_factor, first_y).astype(jnp.bfloat16)
    return running_sum.astype(jnp.bfloat16)


def reorder(rim_cells, seam_code):
    return jnp.where(seam_code == 1, jnp.flip(rim_cells, axis=-1), rim_cells)


def shards(adjoint, section_first, section_second, jacobian, pattern, counts, courant, seam_codes):
    species_dev, levels, rows_dev, seam_len = adjoint.shape
    species_all = jacobian.shape[2]
    block_size = species_all // pattern.shape[2]
    cell_count = rows_dev * seam_len
    first_factor = section_first[0]
    second_factor = section_second[0]
    present = jnp.repeat(jnp.repeat(pattern[0], block_size, axis=1), block_size, axis=2) == 1
    jac_used = jnp.where(present, jacobian[0], jnp.zeros_like(jacobian[0]))
    own_part = adjoint.astype(jnp.bfloat16).reshape(species_dev, levels, cell_count)
    gathered = lax.all_gather(own_part, "spec", axis=0, tiled=True)
    chemistry = section_chain(
        gathered,
        first_factor,
        second_factor,
        jac_used,
        lax.axis_index("spec") * species_dev,
        species_dev,
    )
    cell_index = jnp.arange(cell_count, dtype=jnp.int32)
    active_mask = cell_index[None, :] < counts[0][:, None]
    chem_wide = chemistry.astype(jnp.float32)
    adjoint_flat = adjoint.reshape(species_dev, levels, cell_count)
    adjoint_state = adjoint_flat + jnp.where(
        active_mask[None], chem_wide, jnp.zeros_like(chem_wide)
    )
    adjoint_state = adjoint_state.reshape(species_dev, levels, rows_dev, seam_len)
    upper_code = seam_codes[0, 0]
    lower_code = seam_codes[0, 1]
    seam_row = passed_along(courant[:, -1:, :], "tile", 1)
    lower_faces = jnp.concatenate([reorder(seam_row, lower_code), courant[:, :-1, :]], axis=1)
    rising = jnp.maximum(courant, 0.0)
    falling = jnp.minimum(lower_faces, 0.0)
    for substep in range(NSUB):
        extended = padded(adjoint_state.astype(jnp.bfloat16), (("tile", 2),), 1).astype(
            adjoint_state.dtype
        )
        below_rim = reorder(extended[:, :, :1, :], lower_code)
        above_rim = reorder(extended[:, :, -1:, :], upper_code)
        above_cells = jnp.concatenate([adjoint_state[:, :, 1:, :], above_rim], axis=2)
        below_cells = jnp.concatenate([below_rim, adjoint_state[:, :, :-1, :]], axis=2)
        adjoint_state = (
            adjoint_state
            + rising * (above_cells - adjoint_state)
            + falling * (adjoint_state - below_cells)
        )
    return adjoint_state


def solution(mesh):
    in_specs = (
        P("spec", None, "tile", None),
        P("tile", None, None, None),
        P("tile", None, None, None),
        P("tile", None, None, None),
        P("tile", None, None, None),
        P("tile", None),
        P(None, "tile", None),
        P("tile", None),
    )
    out_specs = P("spec", None, "tile", None)
    return jax.shard_map(shards, mesh=mesh, in_specs=in_specs, out_specs=out_specs, check_vma=False)
```

profile of v0, /device:TPU:1, one launch (start us, length us, event | category | flops | bytes accessed | tf_op | source)
XLA Modules:
  0.0 146.1 jit_solution(7802152960025787586)
XLA Ops:
  6.6 1.2 convert_element_type.91
  8.0 0.8 copy.31
  8.8 4.0 %collective-permute-start.2 = (f32[8,1,128]{2,1,0:T(1,128)S(1)}, f32[8,1,128]{2,1,0:T(1,128)S(1)}, u32[]{:S(2)}, u32[]{:S(2)}) collective-permute-start(f32[8,1,128]{2,1,0:T(1,128)S(1)} %slice.90), channel_id=1, source_target_pairs={{0,4},{4,8},{8,12},{12,16},{16,20},{20,24},{24,28},{28,32},{32,36}... | collective-permute-start | bytes 12296 | tf_op jit(solution)/shard_map/ppermute | solution.py:14
  13.5 1.0 reshape.60
  16.9 9.6 %collective-permute-done.2 = f32[8,1,128]{2,1,0:T(1,128)S(1)} collective-permute-done((f32[8,1,128]{2,1,0:T(1,128)S(1)}, f32[8,1,128]{2,1,0:T(1,128)S(1)}, u32[]{:S(2)}, u32[]{:S(2)}) %collective-permute-start.2) | collective-permute-done | bytes 4128 | tf_op jit(solution)/shard_map/ppermute | solution.py:14
  26.6 23.0 %all-gather.2.cloned.1.call-done = bf16[128,8,512]{2,0,1:T(8,128)(2,1)} async-done(((bf16[32,8,512]{2,0,1:T(8,128)(2,1)}), bf16[128,8,512]{2,0,1:T(8,128)(2,1)}) %all-gather.2.cloned.1.call-update) | async-done | bytes 1048592 | tf_op jit(solution)/shard_map/all_gather | solution.py:71
  49.6 2.7 %fusion.3 = bf16[128,8,512]{0,2,1:T(8,128)(2,1)} fusion(bf16[128,8,512]{2,0,1:T(8,128)(2,1)} %all-gather.2.cloned.1.call-done, bf16[1,8,128,128]{3,2,1,0:T(8,128)(2,1)S(1)} %copy-done), kind=kOutput, calls=%fused_computation.14 | convolution fusion | flops 134742016 | bytes 2359296 | tf_op jit(solution)/shard_map/lsp,slc->plc/dot_general | solution.py:32
  52.3 2.2 %fusion.14 = f32[8,512,128]{1,2,0:T(8,128)S(1)} fusion(bf16[8,128,128]{1,2,0:T(8,128)(2,1)} %bitcast_select_fusion, bf16[128,8,512]{0,2,1:T(8,128)(2,1)} %fusion.3, bf16[1,8,128,128]{3,2,1,0:T(8,128)(2,1)} %param.10), kind=kOutput, calls=%fused_computation.25 | convolution fusion | flops 268959744 | bytes 3670016 | tf_op jit(solution)/shard_map/lsp,slc->plc/dot_general | solution.py:32
  54.5 1.5 %fusion.5 = bf16[128,8,512]{0,2,1:T(8,128)(2,1)} fusion(bf16[128,8,512]{2,0,1:T(8,128)(2,1)S(1)} %copy-done.1, f32[8,512,128]{1,2,0:T(8,128)S(1)} %fusion.14, bf16[1,8,128,128]{3,2,1,0:T(8,128)(2,1)S(1)} %copy-done), kind=kOutput, calls=%fused_computation.16 | convolution fusion | flops 136839168 | bytes 4456448 | tf_op jit(solution)/shard_map/lsp,slc->plc/dot_general | solution.py:32
  56.0 3.4 %fusion.13 = f32[8,512,128]{1,2,0:T(8,128)} fusion(bf16[8,128,128]{1,2,0:T(8,128)(2,1)} %bitcast_select_fusion, bf16[128,8,512]{0,2,1:T(8,128)(2,1)} %fusion.5, bf16[1,8,128,128]{3,2,1,0:T(8,128)(2,1)} %param.10), kind=kOutput, calls=%fused_computation.24 | convolution fusion | flops 268959744 | bytes 3670016 | tf_op jit(solution)/shard_map/lsp,slc->plc/dot_general | solution.py:32
  59.5 3.2 %fusion.7 = bf16[128,8,512]{0,2,1:T(8,128)(2,1)} fusion(bf16[128,8,512]{2,0,1:T(8,128)(2,1)S(1)} %copy-done.1, f32[8,512,128]{1,2,0:T(8,128)} %fusion.13, bf16[1,8,128,128]{3,2,1,0:T(8,128)(2,1)S(1)} %copy-done), kind=kOutput, calls=%fused_computation.18 | convolution fusion | flops 136839168 | bytes 4456448 | tf_op jit(solution)/shard_map/lsp,slc->plc/dot_general | solution.py:32
  62.6 3.4 %fusion.12 = f32[8,512,128]{1,2,0:T(8,128)} fusion(bf16[8,128,128]{1,2,0:T(8,128)(2,1)} %bitcast_select_fusion, bf16[128,8,512]{0,2,1:T(8,128)(2,1)} %fusion.7, bf16[1,8,128,128]{3,2,1,0:T(8,128)(2,1)} %param.10), kind=kOutput, calls=%fused_computation.23 | convolution fusion | flops 268959744 | bytes 3670016 | tf_op jit(solution)/shard_map/lsp,slc->plc/dot_general | solution.py:32
  66.0 3.2 %fusion.9 = bf16[128,8,512]{0,2,1:T(8,128)(2,1)} fusion(bf16[128,8,512]{2,0,1:T(8,128)(2,1)S(1)} %copy-done.1, f32[8,512,128]{1,2,0:T(8,128)} %fusion.12, bf16[1,8,128,128]{3,2,1,0:T(8,128)(2,1)S(1)} %copy-done), kind=kOutput, calls=%fused_computation.20 | convolution fusion | flops 136839168 | bytes 4456448 | tf_op jit(solution)/shard_map/lsp,slc->plc/dot_general | solution.py:32
  69.2 2.7 %fusion.21 = f32[32,8,512]{2,0,1:T(8,128)S(1)} fusion(bf16[128,8,512]{0,2,1:T(8,128)(2,1)} %fusion.9, f32[32,8,512]{2,1,0:T(8,128)} %reshape.60, f32[8,512,128]{1,2,0:T(8,128)} %fusion.12, s32[]{:T(128)S(6)} %select_n.61, f32[8,512,128]{1,2,0:T(8,128)} %fusion.13, f32[8,512,128]{1,2,0:T(8,128)S(1)} %fusion.14, bf16[1,8,128,128]{3,2,1,0:T(8,128)(2,1)} %param.10, ...), kind=kOutput, calls=%fused_computation.32 | convolution fusion | flops 169738240 | bytes 4002816 | tf_op jit(solution)/shard_map/lsp,slc->plc/dot_general | solution.py:32
  72.3 2.2 %collective-permute-start = (bf16[32,8,1,128]{3,2,1,0:T(2,128)(2,1)S(1)}, bf16[32,8,1,128]{3,2,1,0:T(2,128)(2,1)S(1)}, u32[]{:S(2)}, u32[]{:S(2)}) collective-permute-start(bf16[32,8,1,128]{3,2,1,0:T(2,128)(2,1)S(1)} %get-tuple-element.33), channel_id=1, source_target_pairs={{0,4},{4,8},{8,12},{12,16},{16,20},{20,24},{24,28},{28,32},{32,36}... | collective-permute-start | bytes 196616 | tf_op jit(solution)/shard_map/ppermute | solution.py:23
  74.5 9.1 %collective-permute-start.1 = (bf16[32,8,1,128]{3,2,1,0:T(2,128)(2,1)S(1)}, bf16[32,8,1,128]{3,2,1,0:T(2,128)(2,1)S(1)}, u32[]{:S(2)}, u32[]{:S(2)}) collective-permute-start(bf16[32,8,1,128]{3,2,1,0:T(2,128)(2,1)S(1)} %get-tuple-element.34), channel_id=1, source_target_pairs={{4,0},{8,4},{12,8},{16,12},{20,16},{24,20},{28,24},{32,28},{36,32}... | collective-permute-start | bytes 196616 | tf_op jit(solution)/shard_map/ppermute | solution.py:26
  83.9 1.1 collective-permute-done
  85.0 0.9 collective-permute-done.1
  85.9 0.7 maximum_convert_fusion.3
  88.7 1.9 %collective-permute-start.3 = (bf16[32,8,1,128]{3,2,1,0:T(2,128)(2,1)S(1)}, bf16[32,8,1,128]{3,2,1,0:T(2,128)(2,1)S(1)}, u32[]{:S(2)}, u32[]{:S(2)}) collective-permute-start(bf16[32,8,1,128]{3,2,1,0:T(2,128)(2,1)S(1)} %get-tuple-element.31), channel_id=1, source_target_pairs={{0,4},{4,8},{8,12},{12,16},{16,20},{20,24},{24,28},{28,32},{32,36}... | collective-permute-start | bytes 196616 | tf_op jit(solution)/shard_map/ppermute | solution.py:23
  90.6 10.1 %collective-permute-start.4 = (bf16[32,8,1,128]{3,2,1,0:T(2,128)(2,1)S(1)}, bf16[32,8,1,128]{3,2,1,0:T(2,128)(2,1)S(1)}, u32[]{:S(2)}, u32[]{:S(2)}) collective-permute-start(bf16[32,8,1,128]{3,2,1,0:T(2,128)(2,1)S(1)} %get-tuple-element.32), channel_id=1, source_target_pairs={{4,0},{8,4},{12,8},{16,12},{20,16},{24,20},{28,24},{32,28},{36,32}... | collective-permute-start | bytes 196616 | tf_op jit(solution)/shard_map/ppermute | solution.py:26
  101.3 1.4 collective-permute-done.4
  102.7 0.8 maximum_convert_fusion.2
  105.5 1.9 %collective-permute-start.5 = (bf16[32,8,1,128]{3,2,1,0:T(2,128)(2,1)S(1)}, bf16[32,8,1,128]{3,2,1,0:T(2,128)(2,1)S(1)}, u32[]{:S(2)}, u32[]{:S(2)}) collective-permute-start(bf16[32,8,1,128]{3,2,1,0:T(2,128)(2,1)S(1)} %get-tuple-element.29), channel_id=1, source_target_pairs={{0,4},{4,8},{8,12},{12,16},{16,20},{20,24},{24,28},{28,32},{32,36}... | collective-permute-start | bytes 196616 | tf_op jit(solution)/shard_map/ppermute | solution.py:23
  107.5 10.1 %collective-permute-start.6 = (bf16[32,8,1,128]{3,2,1,0:T(2,128)(2,1)S(1)}, bf16[32,8,1,128]{3,2,1,0:T(2,128)(2,1)S(1)}, u32[]{:S(2)}, u32[]{:S(2)}) collective-permute-start(bf16[32,8,1,128]{3,2,1,0:T(2,128)(2,1)S(1)} %get-tuple-element.30), channel_id=1, source_target_pairs={{4,0},{8,4},{12,8},{16,12},{20,16},{24,20},{28,24},{32,28},{36,32}... | collective-permute-start | bytes 196616 | tf_op jit(solution)/shard_map/ppermute | solution.py:26
  117.9 1.4 collective-permute-done.6
  119.3 0.8 maximum_convert_fusion.1
  122.1 1.9 %collective-permute-start.7 = (bf16[32,8,1,128]{3,2,1,0:T(2,128)(2,1)S(1)}, bf16[32,8,1,128]{3,2,1,0:T(2,128)(2,1)S(1)}, u32[]{:S(2)}, u32[]{:S(2)}) collective-permute-start(bf16[32,8,1,128]{3,2,1,0:T(2,128)(2,1)S(1)} %get-tuple-element.27), channel_id=1, source_target_pairs={{0,4},{4,8},{8,12},{12,16},{16,20},{20,24},{24,28},{28,32},{32,36}... | collective-permute-start | bytes 196616 | tf_op jit(solution)/shard_map/ppermute | solution.py:23
  124.1 9.9 %collective-permute-start.8 = (bf16[32,8,1,128]{3,2,1,0:T(2,128)(2,1)S(1)}, bf16[32,8,1,128]{3,2,1,0:T(2,128)(2,1)S(1)}, u32[]{:S(2)}, u32[]{:S(2)}) collective-permute-start(bf16[32,8,1,128]{3,2,1,0:T(2,128)(2,1)S(1)} %get-tuple-element.28), channel_id=1, source_target_pairs={{4,0},{8,4},{12,8},{16,12},{20,16},{24,20},{28,24},{32,28},{36,32}... | collective-permute-start | bytes 196616 | tf_op jit(solution)/shard_map/ppermute | solution.py:26
  134.4 1.5 collective-permute-done.8
  135.9 0.8 fusion.56
  137.9 1.3 fusion.42
  (63 shorter events, 11.4 us)
Async XLA Ops:
  6.5 43.1 %copy-start = (bf16[1,8,128,128]{3,2,1,0:T(8,128)(2,1)S(1)}, bf16[1,8,128,128]{3,2,1,0:T(8,128)(2,1)}, u32[]{:S(2)}) copy-start(bf16[1,8,128,128]{3,2,1,0:T(8,128)(2,1)} %param.9) | copy-start | bytes 786436
  6.5 7.0 %copy-start.2 = (f32[32,8,4,128]{3,2,1,0:T(4,128)S(1)}, f32[32,8,4,128]{3,2,1,0:T(4,128)}, u32[]{:S(2)}) copy-start(f32[32,8,4,128]{3,2,1,0:T(4,128)} %param.8) | copy-start | bytes 1572868
  6.5 2.2 %copy-start.4 = (f32[8,4,128]{2,1,0:T(4,128)S(1)}, f32[8,4,128]{2,1,0:T(4,128)}, u32[]{:S(2)}) copy-start(f32[8,4,128]{2,1,0:T(4,128)} %param.14) | copy-start | bytes 49156
  6.5 6.3 %copy-start.5 = (s32[1,8,2,2]{1,3,2,0:T(2,128)S(1)}, s32[1,8,2,2]{1,3,2,0:T(2,128)}, u32[]{:S(2)}) copy-start(s32[1,8,2,2]{1,3,2,0:T(2,128)} %param.12) | copy-start | bytes 388
  6.5 6.3 %copy-start.7 = (s32[1,8]{1,0:T(1,128)S(1)}, s32[1,8]{1,0:T(1,128)}, u32[]{:S(2)}) copy-start(s32[1,8]{1,0:T(1,128)} %param.13) | copy-start | bytes 100
  6.5 6.4 %copy-start.6 = (s32[1,2]{1,0:T(1,128)S(1)}, s32[1,2]{1,0:T(1,128)}, u32[]{:S(2)}) copy-start(s32[1,2]{1,0:T(1,128)} %param.15) | copy-start | bytes 28
  6.6 8.0 %copy-start.3 = (bf16[1,8,128,128]{3,2,1,0:T(8,128)(2,1)S(1)}, bf16[1,8,128,128]{3,2,1,0:T(8,128)(2,1)}, u32[]{:S(2)}) copy-start(bf16[1,8,128,128]{3,2,1,0:T(8,128)(2,1)} %param.11) | copy-start | bytes 786436
  6.6 43.0 %all-gather.2.cloned.1.call-start = ((), (), s32[]{:S(2)}) async-start(), calls=%async_computation | async-start | bytes 1310720 | tf_op jit(solution)/shard_map/all_gather | solution.py:71
  8.8 17.7 %collective-permute-start.2 = (f32[8,1,128]{2,1,0:T(1,128)S(1)}, f32[8,1,128]{2,1,0:T(1,128)S(1)}, u32[]{:S(2)}, u32[]{:S(2)}) collective-permute-start(f32[8,1,128]{2,1,0:T(1,128)S(1)} %slice.90), channel_id=1, source_target_pairs={{0,4},{4,8},{8,12},{12,16},{16,20},{20,24},{24,28},{28,32},{32,36}... | collective-permute-start | bytes 12296 | tf_op jit(solution)/shard_map/ppermute | solution.py:14
  52.3 2.2 %copy-start.1 = (bf16[128,8,512]{2,0,1:T(8,128)(2,1)S(1)}, bf16[128,8,512]{2,0,1:T(8,128)(2,1)}, u32[]{:S(2)}) copy-start(bf16[128,8,512]{2,0,1:T(8,128)(2,1)} %all-gather.2.cloned.1.call-done) | copy-start | bytes 3145732
  72.3 12.7 %collective-permute-start = (bf16[32,8,1,128]{3,2,1,0:T(2,128)(2,1)S(1)}, bf16[32,8,1,128]{3,2,1,0:T(2,128)(2,1)S(1)}, u32[]{:S(2)}, u32[]{:S(2)}) collective-permute-start(bf16[32,8,1,128]{3,2,1,0:T(2,128)(2,1)S(1)} %get-tuple-element.33), channel_id=1, source_target_pairs={{0,4},{4,8},{8,12},{12,16},{16,20},{20,24},{24,28},{28,32},{32,36}... | collective-permute-start | bytes 196616 | tf_op jit(solution)/shard_map/ppermute | solution.py:23
  74.5 11.4 %collective-permute-start.1 = (bf16[32,8,1,128]{3,2,1,0:T(2,128)(2,1)S(1)}, bf16[32,8,1,128]{3,2,1,0:T(2,128)(2,1)S(1)}, u32[]{:S(2)}, u32[]{:S(2)}) collective-permute-start(bf16[32,8,1,128]{3,2,1,0:T(2,128)(2,1)S(1)} %get-tuple-element.34), channel_id=1, source_target_pairs={{4,0},{8,4},{12,8},{16,12},{20,16},{24,20},{28,24},{32,28},{36,32}... | collective-permute-start | bytes 196616 | tf_op jit(solution)/shard_map/ppermute | solution.py:26
  88.7 12.6 %collective-permute-start.3 = (bf16[32,8,1,128]{3,2,1,0:T(2,128)(2,1)S(1)}, bf16[32,8,1,128]{3,2,1,0:T(2,128)(2,1)S(1)}, u32[]{:S(2)}, u32[]{:S(2)}) collective-permute-start(bf16[32,8,1,128]{3,2,1,0:T(2,128)(2,1)S(1)} %get-tuple-element.31), channel_id=1, source_target_pairs={{0,4},{4,8},{8,12},{12,16},{16,20},{20,24},{24,28},{28,32},{32,36}... | collective-permute-start | bytes 196616 | tf_op jit(solution)/shard_map/ppermute | solution.py:23
  90.6 12.1 %collective-permute-start.4 = (bf16[32,8,1,128]{3,2,1,0:T(2,128)(2,1)S(1)}, bf16[32,8,1,128]{3,2,1,0:T(2,128)(2,1)S(1)}, u32[]{:S(2)}, u32[]{:S(2)}) collective-permute-start(bf16[32,8,1,128]{3,2,1,0:T(2,128)(2,1)S(1)} %get-tuple-element.32), channel_id=1, source_target_pairs={{4,0},{8,4},{12,8},{16,12},{20,16},{24,20},{28,24},{32,28},{36,32}... | collective-permute-start | bytes 196616 | tf_op jit(solution)/shard_map/ppermute | solution.py:26
  105.5 12.4 %collective-permute-start.5 = (bf16[32,8,1,128]{3,2,1,0:T(2,128)(2,1)S(1)}, bf16[32,8,1,128]{3,2,1,0:T(2,128)(2,1)S(1)}, u32[]{:S(2)}, u32[]{:S(2)}) collective-permute-start(bf16[32,8,1,128]{3,2,1,0:T(2,128)(2,1)S(1)} %get-tuple-element.29), channel_id=1, source_target_pairs={{0,4},{4,8},{8,12},{12,16},{16,20},{20,24},{24,28},{28,32},{32,36}... | collective-permute-start | bytes 196616 | tf_op jit(solution)/shard_map/ppermute | solution.py:23
  107.5 11.9 %collective-permute-start.6 = (bf16[32,8,1,128]{3,2,1,0:T(2,128)(2,1)S(1)}, bf16[32,8,1,128]{3,2,1,0:T(2,128)(2,1)S(1)}, u32[]{:S(2)}, u32[]{:S(2)}) collective-permute-start(bf16[32,8,1,128]{3,2,1,0:T(2,128)(2,1)S(1)} %get-tuple-element.30), channel_id=1, source_target_pairs={{4,0},{8,4},{12,8},{16,12},{20,16},{24,20},{28,24},{32,28},{36,32}... | collective-permute-start | bytes 196616 | tf_op jit(solution)/shard_map/ppermute | solution.py:26
  122.1 12.3 %collective-permute-start.7 = (bf16[32,8,1,128]{3,2,1,0:T(2,128)(2,1)S(1)}, bf16[32,8,1,128]{3,2,1,0:T(2,128)(2,1)S(1)}, u32[]{:S(2)}, u32[]{:S(2)}) collective-permute-start(bf16[32,8,1,128]{3,2,1,0:T(2,128)(2,1)S(1)} %get-tuple-element.27), channel_id=1, source_target_pairs={{0,4},{4,8},{8,12},{12,16},{16,20},{20,24},{24,28},{28,32},{32,36}... | collective-permute-start | bytes 196616 | tf_op jit(solution)/shard_map/ppermute | solution.py:23
  124.1 11.8 %collective-permute-start.8 = (bf16[32,8,1,128]{3,2,1,0:T(2,128)(2,1)S(1)}, bf16[32,8,1,128]{3,2,1,0:T(2,128)(2,1)S(1)}, u32[]{:S(2)}, u32[]{:S(2)}) collective-permute-start(bf16[32,8,1,128]{3,2,1,0:T(2,128)(2,1)S(1)} %get-tuple-element.28), channel_id=1, source_target_pairs={{4,0},{8,4},{12,8},{16,12},{20,16},{24,20},{28,24},{32,28},{36,32}... | collective-permute-start | bytes 196616 | tf_op jit(solution)/shard_map/ppermute | solution.py:26
Sparse Core Ops, SparseCore 0:
  9.5 40.0 all-gather.1
where the time goes:
time: 147 us; the launch traced here: 146 us
  starting transfers between devices  51.2 us (35%)
  waiting for transfers between devices  39.2 us (27%)
  matrix products  22.3 us (15%)
  between operations  15 us (10%)
  local copies, waits for them, and re-layouts  9.97 us (7%)
  other arithmetic  8.42 us (6%)
    ppermute x4, starting transfers between devices, padded(): lax.ppermute(lax.slice_in_dim(block, 0, width, axis=dim), axis, backward)  39.2 us
    all_gather x1, waiting for transfers between devices, shards(): gathered = lax.all_gather(own_part, 'spec', axis=0, tiled=True)  23 us
    dot_general x8, matrix products, transposed(): jnp.einsum('lsp,slc->plc', matrix, field_cells, preferred_element_type=jn...  22.3 us
    ppermute x1, waiting for transfers between devices, passed_along(): return lax.ppermute(value, axis, pairs)  9.58 us
    ppermute x4, starting transfers between devices, padded(): lax.ppermute(lax.slice_in_dim(block, block.shape[dim] - width, None, axis...  7.93 us
    ppermute x4, waiting for transfers between devices, padded(): lax.ppermute(lax.slice_in_dim(block, 0, width, axis=dim), axis, backward)  5.19 us
    rev x9, local copies, waits for them, and re-layouts, reorder(): return jnp.where(seam_code == 1, jnp.flip(rim_cells, axis=-1), rim_cells)  4.9 us
    ppermute x1, starting transfers between devices, passed_along(): return lax.ppermute(value, axis, pairs)  4.02 us
  transfers between devices with their start and end apart: 10, of which 9 were waited for; matrix products, arithmetic and copies ran while one was open for 3% of the time, Pallas kernels for 0%

commit v1 on v0

--- a/solution.py
+++ b/solution.py
@@ -1,3 +1,4 @@
+import functools
 import jax
 import jax.numpy as jnp
 from jax import lax
@@ -6,6 +7,18 @@
 NSUB = 4
 section_weights = (0.4, 0.3, 0.2, 0.1)
 coupling = 0.5
+
+
+def draw_the_tails(payload, named_axis):
+    views = []
+    for _ in range(lax.axis_size(named_axis)):
+        views.append(payload)
+    s_next = lax.all_to_all(jnp.stack(views, axis=0), named_axis, 0, 0)
+    block_now = jnp.concatenate(s_next, 0)
+    return block_now
+
+
+form_the_view = functools.partial(draw_the_tails, named_axis="spec")
 
 
 def passed_along(value, axis, steps):
@@ -68,7 +81,7 @@
     present = jnp.repeat(jnp.repeat(pattern[0], block_size, axis=1), block_size, axis=2) == 1
     jac_used = jnp.where(present, jacobian[0], jnp.zeros_like(jacobian[0]))
     own_part = adjoint.astype(jnp.bfloat16).reshape(species_dev, levels, cell_count)
-    gathered = lax.all_gather(own_part, "spec", axis=0, tiled=True)
+    gathered = form_the_view(own_part)
     chemistry = section_chain(
         gathered,
         first_factor,

time: 147 us -> 133 us (0.905)
  the two profiles are of different devices: /device:TPU:1 before, /device:TPU:32 now
where the time goes in v1:
time: 133 us; the launch traced here: 132 us
  starting transfers between devices  62.7 us (47%)
  waiting for transfers between devices  26.6 us (20%)
  matrix products  21.7 us (16%)
  local copies, waits for them, and re-layouts  11 us (8%)
  other arithmetic  8.38 us (6%)
  between operations  1.61 us (1%)
    ppermute x4, starting transfers between devices, padded(): lax.ppermute(lax.slice_in_dim(block, 0, width, axis=dim), axis, backward)  44.2 us
    dot_general x8, matrix products, transposed(): jnp.einsum('lsp,slc->plc', matrix, field_cells, preferred_element_type=jn...  21.7 us
    ppermute x1, waiting for transfers between devices, passed_along(): return lax.ppermute(value, axis, pairs)  16.8 us
    all_to_all x1, starting transfers between devices, draw_the_tails(): s_next = lax.all_to_all(jnp.stack(views, axis=0), named_axis, 0, 0)  8.94 us
    ppermute x4, starting transfers between devices, padded(): lax.ppermute(lax.slice_in_dim(block, block.shape[dim] - width, None, axis...  7.68 us
    rev x9, local copies, waits for them, and re-layouts, reorder(): return jnp.where(seam_code == 1, jnp.flip(rim_cells, axis=-1), rim_cells)  4.9 us
    ppermute x4, waiting for transfers between devices, padded(): lax.ppermute(lax.slice_in_dim(block, block.shape[dim] - width, None, axis...  4.32 us
    ppermute x4, waiting for transfers between devices, padded(): lax.ppermute(lax.slice_in_dim(block, 0, width, axis=dim), axis, backward)  4.3 us
  transfers between devices with their start and end apart: 10, of which 10 were waited for; matrix products, arithmetic and copies ran while one was open for 3% of the time, Pallas kernels for 0%

profile of v1, /device:TPU:32, one launch (start us, length us, event | category | flops | bytes accessed | tf_op | source)
XLA Modules:
  0.0 131.9 jit_solution(13937858685094517536)
XLA Ops:
  0.0 1.2 convert_element_type.91
  1.5 1.1 stack.3
  2.6 8.9 %all-to-all-start = ((bf16[4,32,8,512]{3,1,2,0:T(8,128)(2,1)}), bf16[4,32,8,512]{3,1,2,0:T(8,128)(2,1)S(1)}, u32[]{:S(2)}, u32[]{:S(2)}) async-start(bf16[4,32,8,512]{3,1,2,0:T(8,128)(2,1)} %stack.3), calls=%async_computation | async-start | bytes 2097152 | tf_op jit(solution)/shard_map/all_to_all | solution.py:16
  11.5 1.9 %collective-permute-start.2 = (f32[8,1,128]{2,1,0:T(1,128)S(1)}, f32[8,1,128]{2,1,0:T(1,128)S(1)}, u32[]{:S(2)}, u32[]{:S(2)}) collective-permute-start(f32[8,1,128]{2,1,0:T(1,128)S(1)} %slice.90), channel_id=1, source_target_pairs={{0,4},{4,8},{8,12},{12,16},{16,20},{20,24},{24,28},{28,32},{32,36}... | collective-permute-start | bytes 12296 | tf_op jit(solution)/shard_map/ppermute | solution.py:27
  14.1 1.0 reshape.62
  17.6 16.8 %collective-permute-done.2 = f32[8,1,128]{2,1,0:T(1,128)S(1)} collective-permute-done((f32[8,1,128]{2,1,0:T(1,128)S(1)}, f32[8,1,128]{2,1,0:T(1,128)S(1)}, u32[]{:S(2)}, u32[]{:S(2)}) %collective-permute-start.2) | collective-permute-done | bytes 4128 | tf_op jit(solution)/shard_map/ppermute | solution.py:27
  34.5 1.1 all-to-all-done
  36.2 1.6 %fusion.3 = bf16[128,8,512]{0,2,1:T(8,128)(2,1)} fusion(bf16[128,8,512]{2,1,0:T(8,128)(2,1)S(1)} %bitcast.122, bf16[1,8,128,128]{3,2,1,0:T(8,128)(2,1)S(1)} %copy-done), kind=kOutput, calls=%fused_computation.14 | convolution fusion | flops 134742016 | bytes 2359296 | tf_op jit(solution)/shard_map/lsp,slc->plc/dot_general | solution.py:45
  37.9 2.0 %fusion.14 = f32[8,512,128]{1,2,0:T(8,128)S(1)} fusion(bf16[8,128,128]{1,2,0:T(8,128)(2,1)} %bitcast_select_fusion, bf16[128,8,512]{0,2,1:T(8,128)(2,1)} %fusion.3, bf16[1,8,128,128]{3,2,1,0:T(8,128)(2,1)} %param.10), kind=kOutput, calls=%fused_computation.25 | convolution fusion | flops 268959744 | bytes 3670016 | tf_op jit(solution)/shard_map/lsp,slc->plc/dot_general | solution.py:45
  39.9 1.8 %fusion.5 = bf16[128,8,512]{0,2,1:T(8,128)(2,1)} fusion(f32[8,512,128]{1,2,0:T(8,128)S(1)} %fusion.14, bf16[128,8,512]{2,1,0:T(8,128)(2,1)S(1)} %bitcast.123, bf16[1,8,128,128]{3,2,1,0:T(8,128)(2,1)S(1)} %copy-done), kind=kOutput, calls=%fused_computation.16 | convolution fusion | flops 136839168 | bytes 4456448 | tf_op jit(solution)/shard_map/lsp,slc->plc/dot_general | solution.py:45
  41.7 3.4 %fusion.13 = f32[8,512,128]{1,2,0:T(8,128)} fusion(bf16[8,128,128]{1,2,0:T(8,128)(2,1)} %bitcast_select_fusion, bf16[128,8,512]{0,2,1:T(8,128)(2,1)} %fusion.5, bf16[1,8,128,128]{3,2,1,0:T(8,128)(2,1)} %param.10), kind=kOutput, calls=%fused_computation.24 | convolution fusion | flops 268959744 | bytes 3670016 | tf_op jit(solution)/shard_map/lsp,slc->plc/dot_general | solution.py:45
  45.1 3.4 %fusion.7 = bf16[128,8,512]{0,2,1:T(8,128)(2,1)} fusion(f32[8,512,128]{1,2,0:T(8,128)} %fusion.13, bf16[128,8,512]{2,1,0:T(8,128)(2,1)S(1)} %bitcast.124, bf16[1,8,128,128]{3,2,1,0:T(8,128)(2,1)S(1)} %copy-done), kind=kOutput, calls=%fused_computation.18 | convolution fusion | flops 136839168 | bytes 4456448 | tf_op jit(solution)/shard_map/lsp,slc->plc/dot_general | solution.py:45
  48.5 3.4 %fusion.12 = f32[8,512,128]{1,2,0:T(8,128)} fusion(bf16[8,128,128]{1,2,0:T(8,128)(2,1)} %bitcast_select_fusion, bf16[128,8,512]{0,2,1:T(8,128)(2,1)} %fusion.7, bf16[1,8,128,128]{3,2,1,0:T(8,128)(2,1)} %param.10), kind=kOutput, calls=%fused_computation.23 | convolution fusion | flops 268959744 | bytes 3670016 | tf_op jit(solution)/shard_map/lsp,slc->plc/dot_general | solution.py:45
  51.8 3.4 %fusion.9 = bf16[128,8,512]{0,2,1:T(8,128)(2,1)} fusion(f32[8,512,128]{1,2,0:T(8,128)} %fusion.12, bf16[128,8,512]{2,1,0:T(8,128)(2,1)S(1)} %bitcast.125, bf16[1,8,128,128]{3,2,1,0:T(8,128)(2,1)S(1)} %copy-done), kind=kOutput, calls=%fused_computation.20 | convolution fusion | flops 136839168 | bytes 4456448 | tf_op jit(solution)/shard_map/lsp,slc->plc/dot_general | solution.py:45
  55.2 2.7 %fusion.21 = f32[32,8,512]{2,0,1:T(8,128)S(1)} fusion(bf16[128,8,512]{0,2,1:T(8,128)(2,1)} %fusion.9, f32[32,8,512]{2,1,0:T(8,128)} %reshape.62, f32[8,512,128]{1,2,0:T(8,128)} %fusion.12, s32[]{:T(128)S(6)} %select_n.61, f32[8,512,128]{1,2,0:T(8,128)} %fusion.13, f32[8,512,128]{1,2,0:T(8,128)S(1)} %fusion.14, bf16[1,8,128,128]{3,2,1,0:T(8,128)(2,1)} %param.10, ...), kind=kOutput, calls=%fused_computation.32 | convolution fusion | flops 169738240 | bytes 4002816 | tf_op jit(solution)/shard_map/lsp,slc->plc/dot_general | solution.py:45
  58.3 1.9 %collective-permute-start = (bf16[32,8,1,128]{3,2,1,0:T(2,128)(2,1)S(1)}, bf16[32,8,1,128]{3,2,1,0:T(2,128)(2,1)S(1)}, u32[]{:S(2)}, u32[]{:S(2)}) collective-permute-start(bf16[32,8,1,128]{3,2,1,0:T(2,128)(2,1)S(1)} %get-tuple-element.33), channel_id=1, source_target_pairs={{0,4},{4,8},{8,12},{12,16},{16,20},{20,24},{24,28},{28,32},{32,36}... | collective-permute-start | bytes 196616 | tf_op jit(solution)/shard_map/ppermute | solution.py:36
  60.2 12.7 %collective-permute-start.1 = (bf16[32,8,1,128]{3,2,1,0:T(2,128)(2,1)S(1)}, bf16[32,8,1,128]{3,2,1,0:T(2,128)(2,1)S(1)}, u32[]{:S(2)}, u32[]{:S(2)}) collective-permute-start(bf16[32,8,1,128]{3,2,1,0:T(2,128)(2,1)S(1)} %get-tuple-element.34), channel_id=1, source_target_pairs={{4,0},{8,4},{12,8},{16,12},{20,16},{24,20},{28,24},{32,28},{36,32}... | collective-permute-start | bytes 196616 | tf_op jit(solution)/shard_map/ppermute | solution.py:39
  73.9 1.5 %collective-permute-done.1 = bf16[32,8,1,128]{3,2,1,0:T(2,128)(2,1)S(1)} collective-permute-done((bf16[32,8,1,128]{3,2,1,0:T(2,128)(2,1)S(1)}, bf16[32,8,1,128]{3,2,1,0:T(2,128)(2,1)S(1)}, u32[]{:S(2)}, u32[]{:S(2)}) %collective-permute-start.1) | collective-permute-done | bytes 65568 | tf_op jit(solution)/shard_map/ppermute | solution.py:39
  78.2 1.9 %collective-permute-start.3 = (bf16[32,8,1,128]{3,2,1,0:T(2,128)(2,1)S(1)}, bf16[32,8,1,128]{3,2,1,0:T(2,128)(2,1)S(1)}, u32[]{:S(2)}, u32[]{:S(2)}) collective-permute-start(bf16[32,8,1,128]{3,2,1,0:T(2,128)(2,1)S(1)} %get-tuple-element.31), channel_id=1, source_target_pairs={{0,4},{4,8},{8,12},{12,16},{16,20},{20,24},{24,28},{28,32},{32,36}... | collective-permute-start | bytes 196616 | tf_op jit(solution)/shard_map/ppermute | solution.py:36
  80.2 10.6 %collective-permute-start.4 = (bf16[32,8,1,128]{3,2,1,0:T(2,128)(2,1)S(1)}, bf16[32,8,1,128]{3,2,1,0:T(2,128)(2,1)S(1)}, u32[]{:S(2)}, u32[]{:S(2)}) collective-permute-start(bf16[32,8,1,128]{3,2,1,0:T(2,128)(2,1)S(1)} %get-tuple-element.32), channel_id=1, source_target_pairs={{4,0},{8,4},{12,8},{16,12},{20,16},{24,20},{28,24},{32,28},{36,32}... | collective-permute-start | bytes 196616 | tf_op jit(solution)/shard_map/ppermute | solution.py:39
  91.0 1.1 collective-permute-done.3
  92.1 0.9 collective-permute-done.4
  93.1 0.8 maximum_convert_fusion.2
  95.9 1.9 %collective-permute-start.5 = (bf16[32,8,1,128]{3,2,1,0:T(2,128)(2,1)S(1)}, bf16[32,8,1,128]{3,2,1,0:T(2,128)(2,1)S(1)}, u32[]{:S(2)}, u32[]{:S(2)}) collective-permute-start(bf16[32,8,1,128]{3,2,1,0:T(2,128)(2,1)S(1)} %get-tuple-element.29), channel_id=1, source_target_pairs={{0,4},{4,8},{8,12},{12,16},{16,20},{20,24},{24,28},{28,32},{32,36}... | collective-permute-start | bytes 196616 | tf_op jit(solution)/shard_map/ppermute | solution.py:36
  97.8 10.5 %collective-permute-start.6 = (bf16[32,8,1,128]{3,2,1,0:T(2,128)(2,1)S(1)}, bf16[32,8,1,128]{3,2,1,0:T(2,128)(2,1)S(1)}, u32[]{:S(2)}, u32[]{:S(2)}) collective-permute-start(bf16[32,8,1,128]{3,2,1,0:T(2,128)(2,1)S(1)} %get-tuple-element.30), channel_id=1, source_target_pairs={{4,0},{8,4},{12,8},{16,12},{20,16},{24,20},{28,24},{32,28},{36,32}... | collective-permute-start | bytes 196616 | tf_op jit(solution)/shard_map/ppermute | solution.py:39
  108.6 1.8 %collective-permute-done.5 = bf16[32,8,1,128]{3,2,1,0:T(2,128)(2,1)S(1)} collective-permute-done((bf16[32,8,1,128]{3,2,1,0:T(2,128)(2,1)S(1)}, bf16[32,8,1,128]{3,2,1,0:T(2,128)(2,1)S(1)}, u32[]{:S(2)}, u32[]{:S(2)}) %collective-permute-start.5) | collective-permute-done | bytes 65568 | tf_op jit(solution)/shard_map/ppermute | solution.py:36
  110.8 0.8 maximum_convert_fusion.1
  113.6 1.9 %collective-permute-start.7 = (bf16[32,8,1,128]{3,2,1,0:T(2,128)(2,1)S(1)}, bf16[32,8,1,128]{3,2,1,0:T(2,128)(2,1)S(1)}, u32[]{:S(2)}, u32[]{:S(2)}) collective-permute-start(bf16[32,8,1,128]{3,2,1,0:T(2,128)(2,1)S(1)} %get-tuple-element.27), channel_id=1, source_target_pairs={{0,4},{4,8},{8,12},{12,16},{16,20},{20,24},{24,28},{28,32},{32,36}... | collective-permute-start | bytes 196616 | tf_op jit(solution)/shard_map/ppermute | solution.py:36
  115.6 10.4 %collective-permute-start.8 = (bf16[32,8,1,128]{3,2,1,0:T(2,128)(2,1)S(1)}, bf16[32,8,1,128]{3,2,1,0:T(2,128)(2,1)S(1)}, u32[]{:S(2)}, u32[]{:S(2)}) collective-permute-start(bf16[32,8,1,128]{3,2,1,0:T(2,128)(2,1)S(1)} %get-tuple-element.28), channel_id=1, source_target_pairs={{4,0},{8,4},{12,8},{16,12},{20,16},{24,20},{28,24},{32,28},{36,32}... | collective-permute-start | bytes 196616 | tf_op jit(solution)/shard_map/ppermute | solution.py:39
  127.0 1.5 %collective-permute-done.8 = bf16[32,8,1,128]{3,2,1,0:T(2,128)(2,1)S(1)} collective-permute-done((bf16[32,8,1,128]{3,2,1,0:T(2,128)(2,1)S(1)}, bf16[32,8,1,128]{3,2,1,0:T(2,128)(2,1)S(1)}, u32[]{:S(2)}, u32[]{:S(2)}) %collective-permute-start.8) | collective-permute-done | bytes 65568 | tf_op jit(solution)/shard_map/ppermute | solution.py:39
  128.5 0.8 fusion.60
  130.6 1.3 %fusion.46 = f32[32,8,4,128]{3,2,1,0:T(4,128)} fusion(f32[32,8,4,128]{3,2,1,0:T(4,128)S(1)} %get-tuple-element.6, f32[32,8,1,128]{3,2,1,0:T(1,128)S(1)} %bitcast.135, f32[32,8,3,128]{3,2,1,0:T(4,128)S(1)} %get-tuple-element.14, f32[32,8,3,128]{3,2,1,0:T(4,128)S(1)} %get-tuple-element.13, f32[32,8,1,128]{3,2,1,0:T(1,128)S(1)} %bitcast.134, ...), kind=kLoop, calls=%fused_computation.61 | loop fusion | flops 1048576 | bytes 2129920 | tf_op jit(solution)/shard_map/add | solution.py:116
  (62 shorter events, 14.2 us)
Async XLA Ops:
  0.0 36.2 %copy-start = (bf16[1,8,128,128]{3,2,1,0:T(8,128)(2,1)S(1)}, bf16[1,8,128,128]{3,2,1,0:T(8,128)(2,1)}, u32[]{:S(2)}) copy-start(bf16[1,8,128,128]{3,2,1,0:T(8,128)(2,1)} %param.9) | copy-start | bytes 786436
  1.2 10.3 %copy-start.3 = (f32[8,4,128]{2,1,0:T(4,128)S(1)}, f32[8,4,128]{2,1,0:T(4,128)}, u32[]{:S(2)}) copy-start(f32[8,4,128]{2,1,0:T(4,128)} %param.14) | copy-start | bytes 49156
  1.3 12.1 %copy-start.4 = (s32[1,8,2,2]{1,3,2,0:T(2,128)S(1)}, s32[1,8,2,2]{1,3,2,0:T(2,128)}, u32[]{:S(2)}) copy-start(s32[1,8,2,2]{1,3,2,0:T(2,128)} %param.12) | copy-start | bytes 388
  1.3 12.2 %copy-start.6 = (s32[1,8]{1,0:T(1,128)S(1)}, s32[1,8]{1,0:T(1,128)}, u32[]{:S(2)}) copy-start(s32[1,8]{1,0:T(1,128)} %param.13) | copy-start | bytes 100
  1.3 12.2 %copy-start.5 = (s32[1,2]{1,0:T(1,128)S(1)}, s32[1,2]{1,0:T(1,128)}, u32[]{:S(2)}) copy-start(s32[1,2]{1,0:T(1,128)} %param.15) | copy-start | bytes 28
  1.3 12.8 %copy-start.1 = (f32[32,8,4,128]{3,2,1,0:T(4,128)S(1)}, f32[32,8,4,128]{3,2,1,0:T(4,128)}, u32[]{:S(2)}) copy-start(f32[32,8,4,128]{3,2,1,0:T(4,128)} %param.8) | copy-start | bytes 1572868
  1.4 13.7 %copy-start.2 = (bf16[1,8,128,128]{3,2,1,0:T(8,128)(2,1)S(1)}, bf16[1,8,128,128]{3,2,1,0:T(8,128)(2,1)}, u32[]{:S(2)}) copy-start(bf16[1,8,128,128]{3,2,1,0:T(8,128)(2,1)} %param.11) | copy-start | bytes 786436
  2.6 33.1 %all-to-all-start = ((bf16[4,32,8,512]{3,1,2,0:T(8,128)(2,1)}), bf16[4,32,8,512]{3,1,2,0:T(8,128)(2,1)S(1)}, u32[]{:S(2)}, u32[]{:S(2)}) async-start(bf16[4,32,8,512]{3,1,2,0:T(8,128)(2,1)} %stack.3), calls=%async_computation | async-start | bytes 2097152 | tf_op jit(solution)/shard_map/all_to_all | solution.py:16
  11.5 22.9 %collective-permute-start.2 = (f32[8,1,128]{2,1,0:T(1,128)S(1)}, f32[8,1,128]{2,1,0:T(1,128)S(1)}, u32[]{:S(2)}, u32[]{:S(2)}) collective-permute-start(f32[8,1,128]{2,1,0:T(1,128)S(1)} %slice.90), channel_id=1, source_target_pairs={{0,4},{4,8},{8,12},{12,16},{16,20},{20,24},{24,28},{28,32},{32,36}... | collective-permute-start | bytes 12296 | tf_op jit(solution)/shard_map/ppermute | solution.py:27
  58.3 15.7 %collective-permute-start = (bf16[32,8,1,128]{3,2,1,0:T(2,128)(2,1)S(1)}, bf16[32,8,1,128]{3,2,1,0:T(2,128)(2,1)S(1)}, u32[]{:S(2)}, u32[]{:S(2)}) collective-permute-start(bf16[32,8,1,128]{3,2,1,0:T(2,128)(2,1)S(1)} %get-tuple-element.33), channel_id=1, source_target_pairs={{0,4},{4,8},{8,12},{12,16},{16,20},{20,24},{24,28},{28,32},{32,36}... | collective-permute-start | bytes 196616 | tf_op jit(solution)/shard_map/ppermute | solution.py:36
  60.2 15.2 %collective-permute-start.1 = (bf16[32,8,1,128]{3,2,1,0:T(2,128)(2,1)S(1)}, bf16[32,8,1,128]{3,2,1,0:T(2,128)(2,1)S(1)}, u32[]{:S(2)}, u32[]{:S(2)}) collective-permute-start(bf16[32,8,1,128]{3,2,1,0:T(2,128)(2,1)S(1)} %get-tuple-element.34), channel_id=1, source_target_pairs={{4,0},{8,4},{12,8},{16,12},{20,16},{24,20},{28,24},{32,28},{36,32}... | collective-permute-start | bytes 196616 | tf_op jit(solution)/shard_map/ppermute | solution.py:39
  78.2 13.9 %collective-permute-start.3 = (bf16[32,8,1,128]{3,2,1,0:T(2,128)(2,1)S(1)}, bf16[32,8,1,128]{3,2,1,0:T(2,128)(2,1)S(1)}, u32[]{:S(2)}, u32[]{:S(2)}) collective-permute-start(bf16[32,8,1,128]{3,2,1,0:T(2,128)(2,1)S(1)} %get-tuple-element.31), channel_id=1, source_target_pairs={{0,4},{4,8},{8,12},{12,16},{16,20},{20,24},{24,28},{28,32},{32,36}... | collective-permute-start | bytes 196616 | tf_op jit(solution)/shard_map/ppermute | solution.py:36
  80.2 12.9 %collective-permute-start.4 = (bf16[32,8,1,128]{3,2,1,0:T(2,128)(2,1)S(1)}, bf16[32,8,1,128]{3,2,1,0:T(2,128)(2,1)S(1)}, u32[]{:S(2)}, u32[]{:S(2)}) collective-permute-start(bf16[32,8,1,128]{3,2,1,0:T(2,128)(2,1)S(1)} %get-tuple-element.32), channel_id=1, source_target_pairs={{4,0},{8,4},{12,8},{16,12},{20,16},{24,20},{28,24},{32,28},{36,32}... | collective-permute-start | bytes 196616 | tf_op jit(solution)/shard_map/ppermute | solution.py:39
  95.9 14.5 %collective-permute-start.5 = (bf16[32,8,1,128]{3,2,1,0:T(2,128)(2,1)S(1)}, bf16[32,8,1,128]{3,2,1,0:T(2,128)(2,1)S(1)}, u32[]{:S(2)}, u32[]{:S(2)}) collective-permute-start(bf16[32,8,1,128]{3,2,1,0:T(2,128)(2,1)S(1)} %get-tuple-element.29), channel_id=1, source_target_pairs={{0,4},{4,8},{8,12},{12,16},{16,20},{20,24},{24,28},{28,32},{32,36}... | collective-permute-start | bytes 196616 | tf_op jit(solution)/shard_map/ppermute | solution.py:36
  97.8 13.0 %collective-permute-start.6 = (bf16[32,8,1,128]{3,2,1,0:T(2,128)(2,1)S(1)}, bf16[32,8,1,128]{3,2,1,0:T(2,128)(2,1)S(1)}, u32[]{:S(2)}, u32[]{:S(2)}) collective-permute-start(bf16[32,8,1,128]{3,2,1,0:T(2,128)(2,1)S(1)} %get-tuple-element.30), channel_id=1, source_target_pairs={{4,0},{8,4},{12,8},{16,12},{20,16},{24,20},{28,24},{32,28},{36,32}... | collective-permute-start | bytes 196616 | tf_op jit(solution)/shard_map/ppermute | solution.py:39
  113.6 13.4 %collective-permute-start.7 = (bf16[32,8,1,128]{3,2,1,0:T(2,128)(2,1)S(1)}, bf16[32,8,1,128]{3,2,1,0:T(2,128)(2,1)S(1)}, u32[]{:S(2)}, u32[]{:S(2)}) collective-permute-start(bf16[32,8,1,128]{3,2,1,0:T(2,128)(2,1)S(1)} %get-tuple-element.27), channel_id=1, source_target_pairs={{0,4},{4,8},{8,12},{12,16},{16,20},{20,24},{24,28},{28,32},{32,36}... | collective-permute-start | bytes 196616 | tf_op jit(solution)/shard_map/ppermute | solution.py:36
  115.6 13.0 %collective-permute-start.8 = (bf16[32,8,1,128]{3,2,1,0:T(2,128)(2,1)S(1)}, bf16[32,8,1,128]{3,2,1,0:T(2,128)(2,1)S(1)}, u32[]{:S(2)}, u32[]{:S(2)}) collective-permute-start(bf16[32,8,1,128]{3,2,1,0:T(2,128)(2,1)S(1)} %get-tuple-element.28), channel_id=1, source_target_pairs={{4,0},{8,4},{12,8},{16,12},{20,16},{24,20},{28,24},{32,28},{36,32}... | collective-permute-start | bytes 196616 | tf_op jit(solution)/shard_map/ppermute | solution.py:39
